TPU v7x, 32 devices: a whole 2x2x4 slice. The times are simulated.
32 devices in a mesh: groups: 2 (over x), dev: 8 (over z, y), sub: 2 (over core).
Axes of the slice: x: 2, y: 2, z: 4, core: 2. Of those that a mesh axis runs over, the one named last changes fastest.
Arguments:
- hidden: bfloat16 [128, 6144], P(('groups', 'dev')), parts along dimension 0, may hold values from -6 to 6
- query: bfloat16 [128, 48, 128], P(('groups', 'dev'), 'sub'), parts along dimension 0, may hold values from -180 to 180
- cache_keys: bfloat16 [128, 8, 64, 128], P(('groups', 'dev'), 'sub'), parts along dimension 0, may hold values from -6 to 6
- cache_values: bfloat16 [128, 8, 64, 128], P(('groups', 'dev'), 'sub'), parts along dimension 0, may hold values from -6 to 6
- lengths: int32 [128], P(('groups', 'dev')), parts along dimension 0, may hold values from 16 to 64
- out_proj: bfloat16 [6144, 6144], P('sub', 'dev'), may hold values from -0.078125 to 0.078125
- norm_gain: float32 [6144], replicated, may hold values from 0.1 to 1.9
- router: bfloat16 [6144, 4], replicated, may hold values from -0.078125 to 0.078125
- low_factor: bfloat16 [6144, 256], P('sub'), may hold values from -0.078125 to 0.078125
- gate_weight: bfloat16 [6144, 32768], P(None, ('dev', 'sub')), may hold values from -0.078125 to 0.078125
- up_weight: bfloat16 [6144, 32768], P(None, ('dev', 'sub')), may hold values from -0.078125 to 0.078125
- down_weight: bfloat16 [32768, 6144], P(('dev', 'sub')), may hold values from -0.0625 to 0.0625
- gate_low: bfloat16 [256, 32768], P(None, ('dev', 'sub')), may hold values from -0.375 to 0.375
- up_low: bfloat16 [256, 32768], P(None, ('dev', 'sub')), may hold values from -0.375 to 0.375
- experts: int32 [128, 2], P(('groups', 'dev')), parts along dimension 0, may hold values from 0 to 3, all different within a row; in each aligned block of 8 rows (0 to 7, 8 to 15, ...) at most 6 rows name the same one
Outputs:
- layer_out: bfloat16 [128, 6144], P(('groups', 'dev')), parts along dimension 0
- mixture: float32 [128, 6144], P(('groups', 'dev')), parts along dimension 0
There are 2 independent parts, one for each index of `groups`. A program takes and returns all parts, laid end to end along the dimension named above; an argument that names none is the same for every part. Nothing has to cross between parts.
Inputs may be any that keep to these rules, and one draw needn't show every extreme that they name: Each row names two different experts. Among the 8 requests of one device no expert is named more than 6 times, and that bound is reached on some device.
All inputs are finite; a program needn't handle non-finite values.
Results may differ from a plain program's by a relative error of at most 0.015.
Values may be sent and summed in bfloat16 or wider, within the bound.
A program may use at most 128 MiB of HBM per device.

v0:
```python
import jax
import jax.numpy as jnp
from jax import lax
from jax.sharding import PartitionSpec as P

CAP = 6


EPSILON = 1e-05


def expert_shard(row_block, low_rank, gate_weight, up_weight, down_weight, gate_low, up_low):
    gate_sum = jnp.dot(row_block, gate_weight, preferred_element_type=jnp.float32) + jnp.dot(
        low_rank, gate_low, preferred_element_type=jnp.float32
    )
    up_sum = jnp.dot(row_block, up_weight, preferred_element_type=jnp.float32) + jnp.dot(
        low_rank, up_low, preferred_element_type=jnp.float32
    )
    inner_act = (jax.nn.silu(gate_sum) * up_sum).astype(jnp.bfloat16)
    return jnp.dot(inner_act, down_weight, preferred_element_type=jnp.float32)


def route_gates(normed, router, experts):
    logits = jnp.dot(normed, router, preferred_element_type=jnp.float32)
    labels = lax.broadcasted_iota(jnp.int32, (1, 1, router.shape[1]), 2)
    picked = (experts[:, :, None] == labels).astype(jnp.float32)
    chosen = jnp.sum(logits[:, None, :] * picked, axis=-1)
    leading = jax.nn.sigmoid(chosen[:, 0] - chosen[:, 1])
    return jnp.stack([leading, 1.0 - leading], axis=-1)


def body(
    hidden,
    query,
    cache_keys,
    cache_values,
    lengths,
    out_proj,
    norm_gain,
    router,
    low_factor,
    gate_weight,
    up_weight,
    down_weight,
    gate_low,
    up_low,
    experts,
):
    requests = hidden.shape[0]
    model_width = hidden.shape[1]
    heads_here = query.shape[1]
    kv_here = cache_keys.shape[1]
    span_len = cache_keys.shape[2]
    head_size = query.shape[2]
    grouped = query.reshape(requests, kv_here, heads_here // kv_here, head_size)
    scores = jnp.einsum(
        "rkgd,rkld->rkgl", grouped, cache_keys, preferred_element_type=jnp.float32
    ) * head_size ** (-0.5)
    visible = lax.broadcasted_iota(jnp.int32, (requests, span_len), 1) < lengths[:, None]
    scores = jnp.where(visible[:, None, None, :], scores, -1e30)
    attn_probs = jax.nn.softmax(scores, axis=-1).astype(jnp.bfloat16)
    attended = jnp.einsum(
        "rkgl,rkld->rkgd", attn_probs, cache_values, preferred_element_type=jnp.float32
    )
    attended = attended.astype(jnp.bfloat16).reshape(requests, heads_here * head_size)
    columns = jnp.dot(
        lax.all_gather(attended, "dev", axis=0, tiled=True),
        out_proj,
        preferred_element_type=jnp.float32,
    )
    partial_proj = lax.all_to_all(columns, "dev", split_axis=0, concat_axis=1, tiled=True)
    residual = hidden.astype(jnp.float32) + lax.psum(partial_proj, "sub")
    inverse = lax.rsqrt(jnp.mean(residual * residual, axis=-1, keepdims=True) + EPSILON)
    normed = (residual * inverse * norm_gain).astype(jnp.bfloat16)
    half_width = low_factor.shape[0]
    normed_half = lax.dynamic_slice_in_dim(
        normed, lax.axis_index("sub") * half_width, half_width, 1
    )
    low_partial = jnp.dot(normed_half, low_factor, preferred_element_type=jnp.float32)
    low_rank = lax.psum(low_partial, "sub").astype(jnp.bfloat16)
    rank_width = low_rank.shape[1]
    expert_count = router.shape[1]
    holders = lax.axis_size("dev") // expert_count
    gate_pair = route_gates(normed, router, experts)
    flat_ids = experts.reshape(-1)
    entries = flat_ids.shape[0]
    same_expert = flat_ids[:, None] == flat_ids[None, :]
    earlier = lax.broadcasted_iota(jnp.int32, (entries, entries), 0) > lax.broadcasted_iota(
        jnp.int32, (entries, entries), 1
    )
    slot_index = jnp.sum((same_expert & earlier).astype(jnp.int32), axis=1).reshape(requests, 2)
    target = experts * CAP + slot_index
    placement = (
        target[:, :, None] == lax.broadcasted_iota(jnp.int32, (1, 1, expert_count * CAP), 2)
    ).astype(jnp.float32)
    chosen = jnp.sum(placement, axis=1).astype(jnp.bfloat16)
    packed_rows = jnp.einsum(
        "rs,rd->sd", chosen, normed, preferred_element_type=jnp.float32
    ).astype(jnp.bfloat16)
    packed_low = jnp.einsum(
        "rs,rd->sd", chosen, low_rank, preferred_element_type=jnp.float32
    ).astype(jnp.bfloat16)
    send_rows = jnp.repeat(packed_rows.reshape(expert_count, CAP, model_width), holders, axis=0)
    send_low = jnp.repeat(packed_low.reshape(expert_count, CAP, rank_width), holders, axis=0)
    got_rows = lax.all_to_all(send_rows, "dev", split_axis=0, concat_axis=0, tiled=True)
    got_low = lax.all_to_all(send_low, "dev", split_axis=0, concat_axis=0, tiled=True)
    sources = got_rows.shape[0]
    slot_count = got_rows.shape[1]
    result = expert_shard(
        got_rows.reshape(sources * slot_count, model_width),
        got_low.reshape(sources * slot_count, rank_width),
        gate_weight,
        up_weight,
        down_weight,
        gate_low,
        up_low,
    )
    partials = result.reshape(sources, slot_count, model_width)
    returned = lax.all_to_all(
        partials.astype(jnp.bfloat16), "dev", split_axis=0, concat_axis=0, tiled=True
    ).astype(partials.dtype)
    per_slot = jnp.sum(returned.reshape(expert_count, holders, CAP, model_width), axis=1).reshape(
        expert_count * CAP, model_width
    )
    weighted = jnp.sum(placement * gate_pair[:, :, None], axis=1)
    mixture_part = jnp.dot(weighted, per_slot, precision=lax.Precision.HIGHEST)
    mixture = lax.psum(mixture_part.astype(jnp.bfloat16), "sub").astype(jnp.float32)
    return ((residual + mixture).astype(jnp.bfloat16), mixture)


def solution(mesh):
    placed = (
        P(("groups", "dev"), None),
        P(("groups", "dev"), "sub", None),
        P(("groups", "dev"), "sub", None, None),
        P(("groups", "dev"), "sub", None, None),
        P(("groups", "dev")),
        P("sub", "dev"),
        P(),
        P(),
        P("sub", None),
        P(None, ("dev", "sub")),
        P(None, ("dev", "sub")),
        P(("dev", "sub"), None),
        P(None, ("dev", "sub")),
        P(None, ("dev", "sub")),
        P(("groups", "dev"), None),
    )
    return jax.shard_map(
        body,
        mesh=mesh,
        in_specs=placed,
        out_specs=(P(("groups", "dev"), None), P(("groups", "dev"), None)),
        check_vma=False,
    )
```

profile of v0, /device:TPU:0, one launch (start us, length us, event | category | flops | bytes accessed | tf_op | source)
XLA Modules:
  0.0 208.5 jit_solution(1701919824446412445)
XLA Ops:
  8.8 1.4 fusion.4
  10.5 1.6 convolution_convert_fusion.3
  12.1 32.8 %all_gather.3 = bf16[64,3072]{1,0:T(8,128)(2,1)S(1)} all-gather(bf16[8,3072]{1,0:T(8,128)(2,1)S(1)} %reshape.78), channel_id=1, replica_groups=mesh['groups'=2,'dev'=8,'sub'=2] {'dev'}, dimensions={0}, use_global_device_ids=true | all-gather | bytes 442368 | tf_op jit(solution)/shard_map/all_gather | solution.py:67
  44.9 3.9 %convolution_bitcast_fusion = f32[8,8,768]{2,1,0:T(8,128)} fusion(bf16[64,3072]{1,0:T(8,128)(2,1)S(1)} %all_gather.3, bf16[3072,768]{1,0:T(8,128)(2,1)} %param.20), kind=kOutput, calls=%fused_computation.9 | convolution fusion | flops 301989888 | bytes 5308416 | tf_op jit(solution)/shard_map/dot_general | solution.py:66
  48.8 5.7 %all-to-all-start = ((f32[8,8,768]{2,1,0:T(8,128)}), f32[8,8,768]{2,1,0:T(8,128)S(1)}, u32[]{:S(2)}, u32[]{:S(2)}) async-start(f32[8,8,768]{2,1,0:T(8,128)} %convolution_bitcast_fusion), calls=%async_computation | async-start | bytes 393216 | tf_op jit(solution)/shard_map/all_to_all | solution.py:71
  55.6 6.6 %all-to-all-done = f32[8,8,768]{2,1,0:T(8,128)S(1)} async-done(((f32[8,8,768]{2,1,0:T(8,128)}), f32[8,8,768]{2,1,0:T(8,128)S(1)}, u32[]{:S(2)}, u32[]{:S(2)}) %all-to-all-start) | async-done | bytes 196640 | tf_op jit(solution)/shard_map/all_to_all | solution.py:71
  63.1 16.1 %all-reduce.3.cloned.1.call-done = f32[8,6144]{1,0:T(8,128)} async-done(((f32[8,6144]{1,0:T(8,128)}), f32[8,6144]{1,0:T(8,128)}) %all-reduce.3.cloned.1.call-update) | async-done | bytes 196624 | tf_op jit(solution)/shard_map/psum | solution.py:72
  79.2 1.2 multiply_reduce_fusion
  80.4 1.1 multiply_convert_fusion
  81.5 1.0 fusion.23
  83.5 2.5 %psum.22 = bf16[8,256]{1,0:T(8,128)(2,1)S(1)} all-reduce(f32[8,256]{1,0:T(8,128)S(1)} %fusion.14), channel_id=1, replica_groups=mesh['groups'=2,'dev'=8,'sub'=2] {'sub'}, use_global_device_ids=true, to_apply=%region_8.9 | all-reduce | flops 2048 | bytes 12288 | tf_op jit(solution)/shard_map/psum | solution.py:80
  86.9 5.8 %all-to-all-start.2 = ((bf16[8,6,256]{2,1,0:T(8,128)(2,1)}), bf16[8,6,256]{2,1,0:T(8,128)(2,1)S(1)}, u32[]{:S(2)}, u32[]{:S(2)}) async-start(bf16[8,6,256]{2,1,0:T(8,128)(2,1)} %bitcast.5), calls=%async_computation.2 | async-start | bytes 65536 | tf_op jit(solution)/shard_map/all_to_all | solution.py:106
  93.1 6.3 %all-to-all-done.2 = bf16[8,6,256]{2,1,0:T(8,128)(2,1)S(1)} async-done(((bf16[8,6,256]{2,1,0:T(8,128)(2,1)}), bf16[8,6,256]{2,1,0:T(8,128)(2,1)S(1)}, u32[]{:S(2)}, u32[]{:S(2)}) %all-to-all-start.2) | async-done | bytes 24608 | tf_op jit(solution)/shard_map/all_to_all | solution.py:106
  99.4 0.9 broadcast_in_dim.18
  100.3 3.5 %all-to-all-start.1 = ((bf16[8,6,6144]{2,1,0:T(8,128)(2,1)}), bf16[8,6,6144]{2,1,0:T(8,128)(2,1)S(1)}, u32[]{:S(2)}, u32[]{:S(2)}) async-start(bf16[8,6,6144]{2,1,0:T(8,128)(2,1)} %bitcast.4), calls=%async_computation.1 | async-start | bytes 1572864 | tf_op jit(solution)/shard_map/all_to_all | solution.py:105
  103.9 19.4 %all-to-all-done.1 = bf16[8,6,6144]{2,1,0:T(8,128)(2,1)S(1)} async-done(((bf16[8,6,6144]{2,1,0:T(8,128)(2,1)}), bf16[8,6,6144]{2,1,0:T(8,128)(2,1)S(1)}, u32[]{:S(2)}, u32[]{:S(2)}) %all-to-all-start.1) | async-done | bytes 589856 | tf_op jit(solution)/shard_map/all_to_all | solution.py:105
  123.6 10.5 %fusion.25 = f32[48,2048]{1,0:T(8,128)S(1)} fusion(bf16[48,6144]{1,0:T(8,128)(2,1)S(1)} %reshape.82, bf16[6144,2048]{1,0:T(8,128)(2,1)} %param.25), kind=kOutput, calls=%fused_computation.53 | convolution fusion | flops 1207959552 | bytes 26148864 | tf_op jit(solution)/shard_map/dot_general | solution.py:16
  134.2 10.5 %fusion.24 = f32[48,2048]{1,0:T(8,128)S(1)} fusion(bf16[48,6144]{1,0:T(8,128)(2,1)S(1)} %reshape.82, bf16[6144,2048]{1,0:T(8,128)(2,1)} %param.24), kind=kOutput, calls=%fused_computation.52 | convolution fusion | flops 1207959552 | bytes 26148864 | tf_op jit(solution)/shard_map/dot_general | solution.py:13
  145.1 11.6 %convolution_convert_fusion = bf16[48,6144]{1,0:T(8,128)(2,1)} fusion(bf16[2048,6144]{1,0:T(8,128)(2,1)} %param.26, f32[48,2048]{1,0:T(8,128)S(1)} %fusion.25, bf16[48,256]{1,0:T(8,128)(2,1)S(1)} %reshape.85, bf16[256,2048]{1,0:T(8,128)(2,1)S(1)} %copy-done.2, f32[48,2048]{1,0:T(8,128)S(1)} %convolution_add_fusion.1), kind=kOutput, calls=%fused_computation.1 | convolution fusion | flops 1259274240 | bytes 27615232 | tf_op jit(solution)/shard_map/dot_general | solution.py:20
  156.7 1.3 convert_element_type.62
  158.0 23.6 %all_to_all.34 = bf16[8,6,6144]{2,1,0:T(8,128)(2,1)S(1)} all-to-all(bf16[8,6,6144]{2,1,0:T(8,128)(2,1)S(1)} %convert_element_type.62), channel_id=1, replica_groups=mesh['groups'=2,'dev'=8,'sub'=2] {'dev'}, dimensions={0} | all-to-all | bytes 1179648 | tf_op jit(solution)/shard_map/all_to_all | solution.py:119
  181.8 1.1 convolution_convert_fusion.2
  182.9 17.0 %all-reduce.5.cloned.1.call-done = bf16[8,6144]{1,0:T(8,128)(2,1)} async-done(((bf16[8,6144]{1,0:T(8,128)(2,1)}), bf16[8,6144]{1,0:T(8,128)(2,1)}) %all-reduce.5.cloned.1.call-update) | async-done | bytes 98320 | tf_op jit(solution)/shard_map/psum | solution.py:127
  199.9 1.7 add_convert_fusion
  (42 shorter events, 7.1 us)
Async XLA Ops:
  7.2 76.0 %copy-start = (bf16[3072,256]{1,0:T(8,128)(2,1)S(1)}, bf16[3072,256]{1,0:T(8,128)(2,1)}, u32[]{:S(2)}) copy-start(bf16[3072,256]{1,0:T(8,128)(2,1)} %param.23) | copy-start | bytes 4718596
  48.8 13.4 %all-to-all-start = ((f32[8,8,768]{2,1,0:T(8,128)}), f32[8,8,768]{2,1,0:T(8,128)S(1)}, u32[]{:S(2)}, u32[]{:S(2)}) async-start(f32[8,8,768]{2,1,0:T(8,128)} %convolution_bitcast_fusion), calls=%async_computation | async-start | bytes 393216 | tf_op jit(solution)/shard_map/all_to_all | solution.py:71
  54.5 24.7 %all-reduce.3.cloned.1.call-start = ((), (), s32[]{:S(2)}) async-start(), calls=%async_computation.4 | async-start | bytes 393216 | tf_op jit(solution)/shard_map/psum | solution.py:72
  62.3 0.7 copy-start.5
  86.9 12.5 %all-to-all-start.2 = ((bf16[8,6,256]{2,1,0:T(8,128)(2,1)}), bf16[8,6,256]{2,1,0:T(8,128)(2,1)S(1)}, u32[]{:S(2)}, u32[]{:S(2)}) async-start(bf16[8,6,256]{2,1,0:T(8,128)(2,1)} %bitcast.5), calls=%async_computation.2 | async-start | bytes 65536 | tf_op jit(solution)/shard_map/all_to_all | solution.py:106
  100.3 23.1 %all-to-all-start.1 = ((bf16[8,6,6144]{2,1,0:T(8,128)(2,1)}), bf16[8,6,6144]{2,1,0:T(8,128)(2,1)S(1)}, u32[]{:S(2)}, u32[]{:S(2)}) async-start(bf16[8,6,6144]{2,1,0:T(8,128)(2,1)} %bitcast.4), calls=%async_computation.1 | async-start | bytes 1572864 | tf_op jit(solution)/shard_map/all_to_all | solution.py:105
  103.9 96.1 %all-reduce.5.cloned.1.call-start = ((), (), s32[]{:S(2)}) async-start(), calls=%async_computation.5 | async-start | bytes 196608 | tf_op jit(solution)/shard_map/psum | solution.py:127
  123.6 21.1 %copy-start.3 = (bf16[256,2048]{1,0:T(8,128)(2,1)S(1)}, bf16[256,2048]{1,0:T(8,128)(2,1)}, u32[]{:S(2)}) copy-start(bf16[256,2048]{1,0:T(8,128)(2,1)} %param.27) | copy-start | bytes 3145732
  134.2 10.9 %copy-start.2 = (bf16[256,2048]{1,0:T(8,128)(2,1)S(1)}, bf16[256,2048]{1,0:T(8,128)(2,1)}, u32[]{:S(2)}) copy-start(bf16[256,2048]{1,0:T(8,128)(2,1)} %param.28) | copy-start | bytes 3145732
  144.7 56.9 %copy-start.1 = (bf16[3072,256]{1,0:T(8,128)(2,1)S(1)}, bf16[3072,256]{1,0:T(8,128)(2,1)}, u32[]{:S(2)}) copy-start(bf16[3072,256]{1,0:T(8,128)(2,1)} %param.23) | copy-start | bytes 4718596
  145.1 54.9 %copy-start.4 = (bf16[8,6144]{1,0:T(8,128)(2,1)S(1)}, bf16[8,6144]{1,0:T(8,128)(2,1)}, u32[]{:S(2)}) copy-start(bf16[8,6144]{1,0:T(8,128)(2,1)} %param.15) | copy-start | bytes 294916
Sparse Core Ops, SparseCore 0:
  63.1 16.0 all-reduce.2
  183.0 16.8 all-reduce.4
where the time goes:
time: 209 us; the launch traced here: 208 us
  waiting for transfers between devices  65.5 us (31%)
  blocking collectives  58.9 us (28%)
  matrix products  42.7 us (20%)
  starting transfers between devices  15.1 us (7%)
  between operations  14.2 us (7%)
  other arithmetic  6.22 us (3%)
  local copies, waits for them, and re-layouts  5.86 us (3%)
    all_gather x1, blocking collectives, body(): lax.all_gather(attended, 'dev', axis=0, tiled=True)  32.8 us
    all_to_all x1, blocking collectives, body(): lax.all_to_all(partials.astype(jnp.bfloat16), 'dev', split_axis=0, concat...  23.6 us
    all_to_all x1, waiting for transfers between devices, body(): lax.all_to_all(send_rows, 'dev', split_axis=0, concat_axis=0, tiled=True)  19.4 us
    psum x1, waiting for transfers between devices, body(): lax.psum(mixture_part.astype(jnp.bfloat16), 'sub').astype(jnp.float32)  17 us
    psum x1, waiting for transfers between devices, body(): residual = hidden.astype(jnp.float32) + lax.psum(partial_proj, 'sub')  16.1 us
    dot_general x1, matrix products, expert_shard(): return jnp.dot(inner_act, down_weight, preferred_element_type=jnp.float32)  11.6 us
    dot_general x1, matrix products, expert_shard(): jnp.dot(row_block, up_weight, preferred_element_type=jnp.float32)  10.5 us
    dot_general x1, matrix products, expert_shard(): jnp.dot(row_block, gate_weight, preferred_element_type=jnp.float32)  10.5 us
  transfers between devices with their start and end apart: 5, of which 5 were waited for; matrix products, arithmetic and copies ran while one was open for 1% of the time, Pallas kernels for 0%

commit v1 on v0

--- a/solution.py
+++ b/solution.py
@@ -1,6 +1,10 @@
+import functools
+
 import jax
 import jax.numpy as jnp
 from jax import lax
+from jax.experimental import pallas as pl
+from jax.experimental.pallas import tpu as pltpu
 from jax.sharding import PartitionSpec as P
 
 CAP = 6
@@ -29,7 +33,7 @@
     return jnp.stack([leading, 1.0 - leading], axis=-1)
 
 
-def body(
+def plain_body(
     hidden,
     query,
     cache_keys,
@@ -128,6 +132,558 @@
     return ((residual + mixture).astype(jnp.bfloat16), mixture)
 
 
+CHUNK = 512
+RING_BYTES = 42 * 2**20
+VMEM_BYTES = 66 * 10**6
+F32 = jnp.float32
+BF16 = jnp.bfloat16
+
+
+def layer_kernel(
+    devs,
+    subs,
+    slots,
+    hidden,
+    query,
+    keys,
+    values,
+    lengths,
+    out_proj,
+    gain,
+    router,
+    low_factor,
+    gate_w,
+    up_w,
+    down_w,
+    gate_low,
+    up_low,
+    experts,
+    layer_out,
+    mixture,
+    ring,
+    hid_v,
+    q_v,
+    k_v,
+    v_v,
+    op_v,
+    lf_v,
+    gl_v,
+    ul_v,
+    att_h,
+    att_all,
+    hid_all,
+    exp_all,
+    pair_send,
+    pair_recv,
+    res_all,
+    res32,
+    normed,
+    low_send,
+    low_recv,
+    inner,
+    dsend,
+    drecv,
+    rsend,
+    rrecv,
+    ring_sem,
+    load_sem,
+    bsend_sem,
+    brecv_sem,
+    csend_sem,
+    crecv_sem,
+    asend_sem,
+    arecv_sem,
+    gsend_sem,
+    grecv_sem,
+    fsend_sem,
+    frecv_sem,
+    psend_sem,
+    precv_sem,
+    xsend_sem,
+    xrecv_sem,
+    rs_sem,
+    rr_sem,
+    msend_sem,
+    mrecv_sem,
+):
+    me = lax.axis_index("dev")
+    s = lax.axis_index("sub")
+    mate = 1 - s
+    rows, width = hidden.shape
+    all_rows = devs * rows
+    heads = query.shape[1]
+    kv_here, span, hd = keys.shape[1:]
+    per_kv = heads // kv_here
+    cols = out_proj.shape[1]
+    part = cols // subs
+    units = gate_w.shape[1]
+    depth_blocks = width // units
+    unit_blocks = units // CHUNK
+    per_block = 2 * depth_blocks
+    first_down = unit_blocks * per_block
+    down_steps = width // (2 * CHUNK)
+    total = first_down + 2 * down_steps
+    blocks = devs * subs
+
+    def peer(k):
+        return lax.rem(me + k, devs)
+
+    def remote(src, dst, send_sem, recv_sem, d, sub):
+        return pltpu.make_async_remote_copy(
+            src_ref=src,
+            dst_ref=dst,
+            send_sem=send_sem,
+            recv_sem=recv_sem,
+            device_id={"dev": d, "sub": sub},
+            device_id_type=pl.DeviceIdType.MESH,
+        )
+
+    barrier = pltpu.get_barrier_semaphore()
+    for k in range(1, devs):
+        pl.semaphore_signal(
+            barrier, inc=1, device_id={"dev": peer(k), "sub": s}, device_id_type=pl.DeviceIdType.MESH
+        )
+    pl.semaphore_signal(
+        barrier, inc=1, device_id={"dev": me, "sub": mate}, device_id_type=pl.DeviceIdType.MESH
+    )
+
+    loads = [
+        pltpu.make_async_copy(src, dst, load_sem.at[n])
+        for n, (src, dst) in enumerate(
+            [
+                (query, q_v),
+                (keys, k_v),
+                (values, v_v),
+                (hidden, hid_v),
+                (out_proj, op_v),
+                (low_factor, lf_v),
+                (gate_low, gl_v),
+                (up_low, ul_v),
+            ]
+        )
+    ]
+    for load in loads:
+        load.start()
+
+    def chunk_from(src, row, col, slot):
+        return pltpu.make_async_copy(
+            src.at[pl.ds(row, units), pl.ds(col, CHUNK)], ring.at[slot], ring_sem.at[slot]
+        )
+
+    def down_col(c):
+        pair = c // 2
+        return pl.multiple_of((2 * pair + jnp.where(c % 2 == 0, mate, s)) * CHUNK, CHUNK)
+
+    def start_static(i):
+        slot = i % slots
+        if i < first_down:
+            n, j = divmod(i, per_block)
+            src = gate_w if j < depth_blocks else up_w
+            chunk_from(src, (j % depth_blocks) * units, n * CHUNK, slot).start()
+        else:
+            chunk_from(down_w, 0, down_col(i - first_down), slot).start()
+
+    for i in range(min(slots, total)):
+        start_static(i)
+
+    def refill(i):
+        nxt = i + slots
+        slot = lax.rem(nxt, slots)
+        n = nxt // per_block
+        j = lax.rem(nxt, per_block)
+        col = pl.multiple_of(n * CHUNK, CHUNK)
+
+        @pl.when((nxt < first_down) & (j < depth_blocks))
+        def _():
+            chunk_from(gate_w, pl.multiple_of(j * units, units), col, slot).start()
+
+        @pl.when((nxt < first_down) & (j >= depth_blocks))
+        def _():
+            chunk_from(up_w, pl.multiple_of((j - depth_blocks) * units, units), col, slot).start()
+
+        @pl.when((nxt >= first_down) & (nxt < total))
+        def _():
+            chunk_from(down_w, 0, down_col(nxt - first_down), slot).start()
+
+    def await_chunk(i):
+        slot = lax.rem(i, slots)
+        chunk_from(gate_w, 0, 0, slot).wait()
+        return slot
+
+    lane = lax.broadcasted_iota(jnp.int32, (rows, 128), 1)
+    exp_all[me] = jnp.where(lane == 0, experts[:, 0:1], experts[:, 1:2])
+    loads[3].wait()
+    mine = pl.multiple_of(me * cols + s * part, 128)
+    hid_all[me] = hid_v[:, pl.ds(mine, part)]
+    pl.semaphore_wait(barrier, devs)
+    small = []
+    for k in range(1, devs):
+        p = peer(k)
+        theirs = pl.multiple_of(p * cols + s * part, 128)
+        small.append(
+            remote(exp_all.at[me], exp_all.at[me], bsend_sem.at[k], brecv_sem.at[me], p, s)
+        )
+        small.append(
+            remote(
+                hid_v.at[:, pl.ds(theirs, part)],
+                hid_all.at[me],
+                csend_sem.at[k],
+                crecv_sem.at[me],
+                p,
+                s,
+            )
+        )
+    for copy in small:
+        copy.start()
+
+    for load in loads[:3]:
+        load.wait()
+    at = lax.broadcasted_iota(jnp.int32, (heads, kv_here * span), 1)
+    head = lax.broadcasted_iota(jnp.int32, (heads, kv_here * span), 0)
+    own = (at // span) == (head // per_kv)
+    position = at % span
+    for r in range(rows):
+        scores = (
+            lax.dot_general(
+                q_v[r],
+                k_v[r].reshape(kv_here * span, hd),
+                (((1,), (1,)), ((), ())),
+                preferred_element_type=F32,
+            )
+            * hd ** (-0.5)
+        )
+        scores = jnp.where(own & (position < lengths[r]), scores, -1e30)
+        top = jnp.max(scores, axis=-1, keepdims=True)
+        e = jnp.exp(scores - top)
+        probs = (e / jnp.sum(e, axis=-1, keepdims=True)).astype(BF16)
+        att_h[:, r, :] = jnp.dot(
+            probs, v_v[r].reshape(kv_here * span, hd), preferred_element_type=F32
+        )
+    for h in range(heads):
+        att_all[me, :, h * hd : (h + 1) * hd] = att_h[h].astype(BF16)
+
+    def all_devs(src, dst, send_sem, recv_sem):
+        out = []
+        for k in range(1, devs):
+            copy = remote(src, dst, send_sem.at[k], recv_sem.at[me], peer(k), s)
+            copy.start()
+            out.append(copy)
+        return out
+
+    att_sends = all_devs(att_all.at[me], att_all.at[me], asend_sem, arecv_sem)
+    loads[4].wait()
+    for k in range(1, devs):
+        p = peer(k)
+        remote(att_all.at[p], att_all.at[p], asend_sem.at[k], arecv_sem.at[p], p, s).wait_recv()
+    attended = jnp.concatenate([att_all[d].astype(F32) for d in range(devs)], axis=0).astype(BF16)
+
+    theirs = pl.multiple_of(mate * part, 128)
+    pair_send[...] = jnp.dot(
+        attended, op_v[:, pl.ds(theirs, part)], preferred_element_type=F32
+    )
+    pair_copy = remote(pair_send, pair_recv, psend_sem.at[0], precv_sem.at[0], me, mate)
+    pair_copy.start()
+    ours = pl.multiple_of(s * part, 128)
+    projected = jnp.dot(attended, op_v[:, pl.ds(ours, part)], preferred_element_type=F32)
+    for k in range(1, devs):
+        p = peer(k)
+        remote(exp_all.at[p], exp_all.at[p], bsend_sem.at[k], brecv_sem.at[p], p, s).wait_recv()
+        remote(
+            hid_all.at[p], hid_all.at[p], csend_sem.at[k], crecv_sem.at[p], p, s
+        ).wait_recv()
+    own_hidden = jnp.concatenate([hid_all[d].astype(F32) for d in range(devs)], axis=0)
+    pair_copy.wait_recv()
+    my_block = me * subs + s
+    res_all[my_block] = (own_hidden + (projected + pair_recv[...])).astype(BF16)
+
+    res_sends = []
+    copy = remote(
+        res_all.at[my_block],
+        res_all.at[my_block],
+        fsend_sem.at[0],
+        frecv_sem.at[me],
+        me,
+        mate,
+    )
+    for k in range(1, devs):
+        c = remote(
+            res_all.at[my_block],
+            res_all.at[my_block],
+            gsend_sem.at[k],
+            grecv_sem.at[me],
+            peer(k),
+            s,
+        )
+        c.start()
+        res_sends.append(c)
+    copy.start()
+    res_sends.append(copy)
+    for k in range(1, devs):
+        p = peer(k)
+        b = p * subs + s
+        remote(res_all.at[b], res_all.at[b], gsend_sem.at[k], grecv_sem.at[p], p, s).wait_recv()
+        c = remote(res_all.at[b], res_all.at[b], fsend_sem.at[k], frecv_sem.at[p], me, mate)
+        c.start()
+        res_sends.append(c)
+    for k in range(devs):
+        p = peer(k)
+        b = p * subs + mate
+        remote(res_all.at[b], res_all.at[b], fsend_sem.at[k], frecv_sem.at[p], me, mate).wait_recv()
+
+    squares = jnp.zeros((all_rows, 1), F32)
+    for b in range(blocks):
+        x = res_all[b].astype(F32)
+        res32[:, b * part : (b + 1) * part] = x
+        squares = squares + jnp.sum(x * x, axis=-1, keepdims=True)
+    inverse = lax.rsqrt(squares / width + EPSILON)
+    for b in range(blocks):
+        at_cols = slice(b * part, (b + 1) * part)
+        normed[:, at_cols] = (res32[:, at_cols] * inverse * gain[:, at_cols]).astype(BF16)
+
+    half = low_factor.shape[0]
+    loads[5].wait()
+    low_send[...] = jnp.dot(
+        normed[:, pl.ds(pl.multiple_of(s * half, 128), half)], lf_v[...], preferred_element_type=F32
+    )
+    low_copy = remote(low_send, low_recv, psend_sem.at[1], precv_sem.at[1], me, mate)
+    low_copy.start()
+
+    logits = lax.dot_general(
+        normed[...], router[...], (((1,), (1,)), ((), ())), preferred_element_type=F32
+    )
+    count = router.shape[0]
+    label = lax.broadcasted_iota(jnp.int32, (all_rows, count), 1)
+    named = exp_all[...].reshape(all_rows, 128)
+    e0 = named[:, 0:1]
+    e1 = named[:, 1:2]
+    a = jnp.sum(jnp.where(label == e0, logits, 0.0), axis=-1, keepdims=True)
+    b = jnp.sum(jnp.where(label == e1, logits, 0.0), axis=-1, keepdims=True)
+    lead = jax.nn.sigmoid(a - b)
+    here = me // (devs // count)
+    share = jnp.where(e0 == here, lead, 0.0) + jnp.where(e1 == here, 1.0 - lead, 0.0)
+
+    loads[6].wait()
+    loads[7].wait()
+    low_copy.wait_recv()
+    low = (low_send[...] + low_recv[...]).astype(BF16)
+
+    def unit_step(n, carry):
+        at_units = pl.ds(pl.multiple_of(n * CHUNK, CHUNK), CHUNK)
+        gate_sum = jnp.dot(low, gl_v[:, at_units], preferred_element_type=F32)
+        up_sum = jnp.dot(low, ul_v[:, at_units], preferred_element_type=F32)
+        for j in range(depth_blocks):
+            i = n * per_block + j
+            slot = await_chunk(i)
+            gate_sum += jnp.dot(
+                normed[:, j * units : (j + 1) * units], ring[slot], preferred_element_type=F32
+            )
+            refill(i)
+        for j in range(depth_blocks):
+            i = n * per_block + depth_blocks + j
+            slot = await_chunk(i)
+            up_sum += jnp.dot(
+                normed[:, j * units : (j + 1) * units], ring[slot], preferred_element_type=F32
+            )
+            refill(i)
+        inner[:, at_units] = (gate_sum / (1.0 + jnp.exp(-gate_sum)) * up_sum).astype(BF16)
+        return carry
+
+    lax.fori_loop(0, unit_blocks, unit_step, 0)
+
+    def down_step(c, carry):
+        i = first_down + 2 * c
+        slot = await_chunk(i)
+        dsend[c] = (
+            jnp.dot(inner[...], ring[slot], preferred_element_type=F32) * share
+        ).astype(BF16)
+        remote(dsend.at[c], drecv.at[c], xsend_sem.at[c], xrecv_sem.at[c], me, mate).start()
+        refill(i)
+        slot = await_chunk(i + 1)
+        y = jnp.dot(inner[...], ring[slot], preferred_element_type=F32) * share
+        refill(i + 1)
+        remote(dsend.at[c], drecv.at[c], xsend_sem.at[c], xrecv_sem.at[c], me, mate).wait_recv()
+        y = y + drecv[c].astype(F32)
+        for d in range(devs):
+            rsend[c, d] = y[d * rows : (d + 1) * rows].astype(BF16)
+        rrecv[c, me] = rsend[c, me]
+        for k in range(1, devs):
+            p = peer(k)
+            remote(
+                rsend.at[c, p], rrecv.at[c, me], rs_sem.at[c, k], rr_sem.at[c, me], p, s
+            ).start()
+        return carry
+
+    lax.fori_loop(0, down_steps, down_step, 0)
+
+    def sum_step(c, carry):
+        for k in range(1, devs):
+            p = peer(k)
+            remote(
+                rsend.at[c, p], rrecv.at[c, p], rs_sem.at[c, k], rr_sem.at[c, p], p, s
+            ).wait_recv()
+        got = rrecv[c, 0].astype(F32)
+        for d in range(1, devs):
+            got = got + rrecv[c, d].astype(F32)
+        at_cols = pl.ds(pl.multiple_of((2 * c + s) * CHUNK, CHUNK), CHUNK)
+        mixture[:, at_cols] = got
+        remote(
+            mixture.at[:, at_cols],
+            mixture.at[:, at_cols],
+            msend_sem.at[c],
+            mrecv_sem.at[c],
+            me,
+            mate,
+        ).start()
+        return carry
+
+    lax.fori_loop(0, down_steps, sum_step, 0)
+
+    def last_step(c, carry):
+        at_cols = pl.ds(pl.multiple_of((2 * c + mate) * CHUNK, CHUNK), CHUNK)
+        swap = remote(
+            mixture.at[:, at_cols],
+            mixture.at[:, at_cols],
+            msend_sem.at[c],
+            mrecv_sem.at[c],
+            me,
+            mate,
+        )
+        swap.wait()
+        remote(dsend.at[c], drecv.at[c], xsend_sem.at[c], xrecv_sem.at[c], me, mate).wait_send()
+        for k in range(1, devs):
+            p = peer(k)
+            remote(
+                rsend.at[c, p], rrecv.at[c, me], rs_sem.at[c, k], rr_sem.at[c, me], p, s
+            ).wait_send()
+        return carry
+
+    lax.fori_loop(0, down_steps, last_step, 0)
+    my_rows = pl.ds(pl.multiple_of(me * rows, rows), rows)
+    layer_out[...] = (res32[my_rows, :] + mixture[...]).astype(BF16)
+    for copy in small + att_sends + res_sends + [pair_copy, low_copy]:
+        copy.wait_send()
+
+
+def fits(mesh, shapes):
+    devs, subs = mesh.shape["dev"], mesh.shape["sub"]
+    hidden, query, keys, out_proj, router, gate_w = shapes
+    width = hidden[1]
+    units = gate_w[1]
+    return (
+        subs == 2
+        and devs * hidden[0] <= 128
+        and hidden[0] == 8
+        and query[2] == 128
+        and out_proj[1] % (128 * subs) == 0
+        and units % CHUNK == 0
+        and width % units == 0
+        and width % (2 * CHUNK) == 0
+        and devs % router[1] == 0
+    )
+
+
+def body(mesh, *args):
+    (
+        hidden,
+        query,
+        keys,
+        values,
+        lengths,
+        out_proj,
+        gain,
+        router,
+        low_factor,
+        gate_w,
+        up_w,
+        down_w,
+        gate_low,
+        up_low,
+        experts,
+    ) = args
+    shapes = [x.shape for x in (hidden, query, keys, out_proj, router, gate_w)]
+    if not fits(mesh, shapes):
+        return plain_body(*args)
+    devs, subs = mesh.shape["dev"], mesh.shape["sub"]
+    rows, width = hidden.shape
+    all_rows = devs * rows
+    heads, hd = query.shape[1:]
+    part = out_proj.shape[1] // subs
+    units = gate_w.shape[1]
+    rank = low_factor.shape[1]
+    down_steps = width // (2 * CHUNK)
+    total = 2 * (width // units) * (units // CHUNK) + 2 * down_steps
+    slots = min(total, RING_BYTES // (units * CHUNK * 2))
+    anywhere = pl.BlockSpec(memory_space=pl.ANY)
+    vmem = pl.BlockSpec(memory_space=pltpu.VMEM)
+    smem = pl.BlockSpec(memory_space=pltpu.SMEM)
+    dma = pltpu.SemaphoreType.DMA
+    scratch = [
+        pltpu.VMEM((slots, units, CHUNK), BF16),
+        pltpu.VMEM(hidden.shape, BF16),
+        pltpu.VMEM(query.shape, BF16),
+        pltpu.VMEM(keys.shape, BF16),
+        pltpu.VMEM(values.shape, BF16),
+        pltpu.VMEM(out_proj.shape, BF16),
+        pltpu.VMEM(low_factor.shape, BF16),
+        pltpu.VMEM(gate_low.shape, BF16),
+        pltpu.VMEM(up_low.shape, BF16),
+        pltpu.VMEM((heads, rows, hd), F32),
+        pltpu.VMEM((devs, rows, heads * hd), BF16),
+        pltpu.VMEM((devs, rows, part), BF16),
+        pltpu.VMEM((devs, rows, 128), jnp.int32),
+        pltpu.VMEM((all_rows, part), F32),
+        pltpu.VMEM((all_rows, part), F32),
+        pltpu.VMEM((devs * subs, all_rows, part), BF16),
+        pltpu.VMEM((all_rows, width), F32),
+        pltpu.VMEM((all_rows, width), BF16),
+        pltpu.VMEM((all_rows, rank), F32),
+        pltpu.VMEM((all_rows, rank), F32),
+        pltpu.VMEM((all_rows, units), BF16),
+        pltpu.VMEM((down_steps, all_rows, CHUNK), BF16),
+        pltpu.VMEM((down_steps, all_rows, CHUNK), BF16),
+        pltpu.VMEM((down_steps, devs, rows, CHUNK), BF16),
+        pltpu.VMEM((down_steps, devs, rows, CHUNK), BF16),
+        dma((slots,)),
+        dma((8,)),
+    ]
+    scratch += [dma((devs,)) for _ in range(10)]
+    scratch += [dma((2,)), dma((2,)), dma((down_steps,)), dma((down_steps,))]
+    scratch += [dma((down_steps, devs)), dma((down_steps, devs))]
+    scratch += [dma((down_steps,)), dma((down_steps,))]
+    return pl.pallas_call(
+        functools.partial(layer_kernel, devs, subs, slots),
+        out_shape=(
+            jax.ShapeDtypeStruct((rows, width), BF16),
+            jax.ShapeDtypeStruct((rows, width), F32),
+        ),
+        in_specs=[anywhere] * 4
+        + [smem, anywhere, vmem, vmem]
+        + [anywhere] * 6
+        + [vmem],
+        out_specs=(vmem, vmem),
+        scratch_shapes=scratch,
+        compiler_params=pltpu.CompilerParams(
+            collective_id=0, has_side_effects=True, vmem_limit_bytes=VMEM_BYTES
+        ),
+    )(
+        hidden,
+        query,
+        keys,
+        values,
+        lengths,
+        out_proj,
+        gain.reshape(1, width),
+        router.T,
+        low_factor,
+        gate_w,
+        up_w,
+        down_w,
+        gate_low,
+        up_low,
+        experts,
+    )
+
+
 def solution(mesh):
     placed = (
         P(("groups", "dev"), None),
@@ -147,7 +703,7 @@
         P(("groups", "dev"), None),
     )
     return jax.shard_map(
-        body,
+        functools.partial(body, mesh),
         mesh=mesh,
         in_specs=placed,
         out_specs=(P(("groups", "dev"), None), P(("groups", "dev"), None)),

time: 209 us -> 77.3 us (0.37)
  Pallas kernels: 0 us -> 72 us
  waiting for transfers between devices: 65.5 us -> 0 us
  blocking collectives: 58.9 us -> 0 us
  matrix products: 42.7 us -> 0 us
  starting transfers between devices: 15.1 us -> 0 us
  between operations: 14.2 us -> 0.64 us
  other arithmetic: 6.22 us -> 0 us
    pallas_call x0 -> x1, Pallas kernels: none -> 72 us  [body(): pl.pallas_call(functools.partial(layer_kernel, devs, subs, slots), out_sh...]
    dot_general x12 -> x0, matrix products: 42.7 us -> none  [the longest x1 11.6 us: expert_shard(): return jnp.dot(inner_act, down_weight, preferred_element_type=jnp.float32)]
    psum x2 -> x0, waiting for transfers between devices: 33.2 us -> none  [the longest x1 17 us: body(): lax.psum(mixture_part.astype(jnp.bfloat16), 'sub').astype(jnp.float32)]
    all_gather x1 -> x0, blocking collectives: 32.8 us -> none  [body(): lax.all_gather(attended, 'dev', axis=0, tiled=True)]
    all_to_all x3 -> x0, waiting for transfers between devices: 32.4 us -> none  [the longest x1 19.4 us: body(): lax.all_to_all(send_rows, 'dev', split_axis=0, concat_axis=0, tiled=True)]
    all_to_all x1 -> x0, blocking collectives: 23.6 us -> none  [body(): lax.all_to_all(partials.astype(jnp.bfloat16), 'dev', split_axis=0, concat...]
    all_to_all x3 -> x0, starting transfers between devices: 15 us -> none  [the longest x1 5.82 us: body(): lax.all_to_all(send_low, 'dev', split_axis=0, concat_axis=0, tiled=True)]
    convert_element_type x2 -> x0, other arithmetic: 2.83 us -> none  [the longest x1 1.72 us: body(): return ((residual + mixture).astype(jnp.bfloat16), mixture)]
  transfers between devices with their start and end apart: 5 -> 0, of which waited for: 5 -> 0; matrix products, arithmetic and copies ran while one was open for 1% -> 0% of each run, Pallas kernels for 0% -> 0%
where the time goes in v1:
time: 77.3 us; the launch traced here: 77.1 us
  Pallas kernels  72 us (93%)
  local copies, waits for them, and re-layouts  4.5 us (6%)
    pallas_call x1, Pallas kernels, body(): pl.pallas_call(functools.partial(layer_kernel, devs, subs, slots), out_sh...  72 us
    unnamed x3, local copies, waits for them, and re-layouts  4.5 us

profile of v1, /device:TPU:0, one launch (start us, length us, event | category | flops | bytes accessed | tf_op | source)
XLA Modules:
  0.0 77.1 jit_solution(5882731569375124166)
XLA Ops:
  0.6 1.3 %copy.17.experts = s32[8,2]{1,0:T(8,128)} copy(s32[8,2]{0,1:T(2,128)} %param.29) | data formatting | bytes 128 | tf_op args[14]
  2.0 72.0 %shard_map.158 = (bf16[8,6144]{1,0:T(8,128)(2,1)}, f32[8,6144]{1,0:T(8,128)}) custom-call(bf16[8,6144]{1,0:T(8,128)(2,1)} %hidden.1, bf16[8,24,128]{2,1,0:T(8,128)(2,1)} %query.1, bf16[8,4,64,128]{3,2,1,0:T(8,128)(2,1)} %keys.1, bf16[8,4,64,128]{3,2,1,0:T(8,128)(2,1)} %values.1, s32[8]{0:T(128)} %lengths.1, bf16[3072,768]{1,0:T(8,128)(2,1)} %out_proj.1, ...), custom_call_target="tpu_custom_call" | custom-call | tf_op jit(solution)/shard_map/pallas_call | solution.py:653
  73.9 1.5 %copy.20 = bf16[8,6144]{1,0:T(8,128)(2,1)} copy(bf16[8,6144]{1,0:T(8,128)(2,1)} %get-tuple-element.4) | data formatting | bytes 196608
  75.5 1.6 %copy.21 = f32[8,6144]{1,0:T(8,128)} copy(f32[8,6144]{1,0:T(8,128)} %get-tuple-element.5) | data formatting | bytes 393216

commit v2 on v1

--- a/solution.py
+++ b/solution.py
@@ -133,8 +133,10 @@
 
 
 CHUNK = 512
+NEAR = 2
 RING_BYTES = 42 * 2**20
 VMEM_BYTES = 66 * 10**6
+STAGES = (0, 8, 16)
 F32 = jnp.float32
 BF16 = jnp.bfloat16
 
@@ -158,7 +160,7 @@
     gate_low,
     up_low,
     experts,
-    layer_out,
+    residual,
     mixture,
     ring,
     hid_v,
@@ -181,6 +183,7 @@
     low_send,
     low_recv,
     inner,
+    kept,
     dsend,
     drecv,
     rsend,
@@ -283,8 +286,12 @@
         else:
             chunk_from(down_w, 0, down_col(i - first_down), slot).start()
 
-    for i in range(min(slots, total)):
-        start_static(i)
+    def prefetch(stage):
+        for i in range(slots):
+            if sum(i >= edge * slots // 20 for edge in STAGES) == stage:
+                start_static(i)
+
+    prefetch(0)
 
     def refill(i):
         nxt = i + slots
@@ -311,7 +318,11 @@
         return slot
 
     lane = lax.broadcasted_iota(jnp.int32, (rows, 128), 1)
-    exp_all[me] = jnp.where(lane == 0, experts[:, 0:1], experts[:, 1:2])
+    row = lax.broadcasted_iota(jnp.int32, (rows, 128), 0)
+    named = jnp.zeros((rows, 128), jnp.int32)
+    for r in range(rows):
+        named = jnp.where(row == r, jnp.where(lane == 0, experts[0, r], experts[1, r]), named)
+    exp_all[me] = named
     loads[3].wait()
     mine = pl.multiple_of(me * cols + s * part, 128)
     hid_all[me] = hid_v[:, pl.ds(mine, part)]
@@ -362,19 +373,42 @@
     for h in range(heads):
         att_all[me, :, h * hd : (h + 1) * hd] = att_h[h].astype(BF16)
 
-    def all_devs(src, dst, send_sem, recv_sem):
+    far = devs // NEAR
+    beside = me + 1 - 2 * lax.rem(me, NEAR)
+
+    def far_peer(k):
+        return lax.rem(me + NEAR * k, devs)
+
+    def gather_start(buf, index, send_sem, recv_sem):
+        block = buf.at[index(me)]
         out = []
-        for k in range(1, devs):
-            copy = remote(src, dst, send_sem.at[k], recv_sem.at[me], peer(k), s)
+        for k in range(1, far):
+            out.append(remote(block, block, send_sem.at[k], recv_sem.at[me], far_peer(k), s))
+        out.append(remote(block, block, send_sem.at[far], recv_sem.at[me], beside, s))
+        for copy in out:
+            copy.start()
+        return out
+
+    def gather_finish(buf, index, send_sem, recv_sem, out, arrived):
+        for k in range(1, far):
+            p = far_peer(k)
+            block = buf.at[index(p)]
+            remote(block, block, send_sem.at[k], recv_sem.at[p], p, s).wait_recv()
+            copy = remote(block, block, send_sem.at[far + k], recv_sem.at[p], beside, s)
             copy.start()
             out.append(copy)
-        return out
-
-    att_sends = all_devs(att_all.at[me], att_all.at[me], asend_sem, arecv_sem)
+            arrived(p, k)
+        for k in range(far):
+            p = lax.rem(beside + NEAR * k, devs)
+            block = buf.at[index(p)]
+            remote(block, block, send_sem.at[far], recv_sem.at[p], beside, s).wait_recv()
+            arrived(p, far + k)
+
+    same = lambda p: p
+    att_sends = gather_start(att_all, same, asend_sem, arecv_sem)
+    prefetch(1)
+    gather_finish(att_all, same, asend_sem, arecv_sem, att_sends, lambda p, k: None)
     loads[4].wait()
-    for k in range(1, devs):
-        p = peer(k)
-        remote(att_all.at[p], att_all.at[p], asend_sem.at[k], arecv_sem.at[p], p, s).wait_recv()
     attended = jnp.concatenate([att_all[d].astype(F32) for d in range(devs)], axis=0).astype(BF16)
 
     theirs = pl.multiple_of(mate * part, 128)
@@ -396,39 +430,25 @@
     my_block = me * subs + s
     res_all[my_block] = (own_hidden + (projected + pair_recv[...])).astype(BF16)
 
-    res_sends = []
-    copy = remote(
-        res_all.at[my_block],
-        res_all.at[my_block],
-        fsend_sem.at[0],
-        frecv_sem.at[me],
-        me,
-        mate,
-    )
-    for k in range(1, devs):
-        c = remote(
-            res_all.at[my_block],
-            res_all.at[my_block],
-            gsend_sem.at[k],
-            grecv_sem.at[me],
-            peer(k),
-            s,
-        )
-        c.start()
-        res_sends.append(c)
-    copy.start()
-    res_sends.append(copy)
-    for k in range(1, devs):
-        p = peer(k)
-        b = p * subs + s
-        remote(res_all.at[b], res_all.at[b], gsend_sem.at[k], grecv_sem.at[p], p, s).wait_recv()
-        c = remote(res_all.at[b], res_all.at[b], fsend_sem.at[k], frecv_sem.at[p], me, mate)
-        c.start()
-        res_sends.append(c)
+    def block_of(p):
+        return p * subs + s
+
+    res_sends = gather_start(res_all, block_of, gsend_sem, grecv_sem)
+
+    def over(p, k):
+        block = res_all.at[block_of(p)]
+        copy = remote(block, block, fsend_sem.at[k], frecv_sem.at[p], me, mate)
+        copy.start()
+        res_sends.append(copy)
+
+    over(me, 0)
+    prefetch(2)
+    gather_finish(res_all, block_of, gsend_sem, grecv_sem, res_sends, over)
     for k in range(devs):
         p = peer(k)
-        b = p * subs + mate
-        remote(res_all.at[b], res_all.at[b], fsend_sem.at[k], frecv_sem.at[p], me, mate).wait_recv()
+        block = res_all.at[p * subs + mate]
+        remote(block, block, fsend_sem.at[k], frecv_sem.at[p], me, mate).wait_recv()
+    prefetch(3)
 
     squares = jnp.zeros((all_rows, 1), F32)
     for b in range(blocks):
@@ -490,6 +510,18 @@
 
     lax.fori_loop(0, unit_blocks, unit_step, 0)
 
+    def give_back(c):
+        remote(dsend.at[c], drecv.at[c], xsend_sem.at[c], xrecv_sem.at[c], me, mate).wait_recv()
+        y = kept[c % 2] + drecv[c].astype(F32)
+        for d in range(devs):
+            rsend[c, d] = y[d * rows : (d + 1) * rows].astype(BF16)
+        rrecv[c, me] = rsend[c, me]
+        for k in range(1, devs):
+            p = peer(k)
+            remote(
+                rsend.at[c, p], rrecv.at[c, me], rs_sem.at[c, k], rr_sem.at[c, me], p, s
+            ).start()
+
     def down_step(c, carry):
         i = first_down + 2 * c
         slot = await_chunk(i)
@@ -499,21 +531,17 @@
         remote(dsend.at[c], drecv.at[c], xsend_sem.at[c], xrecv_sem.at[c], me, mate).start()
         refill(i)
         slot = await_chunk(i + 1)
-        y = jnp.dot(inner[...], ring[slot], preferred_element_type=F32) * share
+        kept[lax.rem(c, 2)] = jnp.dot(inner[...], ring[slot], preferred_element_type=F32) * share
         refill(i + 1)
-        remote(dsend.at[c], drecv.at[c], xsend_sem.at[c], xrecv_sem.at[c], me, mate).wait_recv()
-        y = y + drecv[c].astype(F32)
-        for d in range(devs):
-            rsend[c, d] = y[d * rows : (d + 1) * rows].astype(BF16)
-        rrecv[c, me] = rsend[c, me]
-        for k in range(1, devs):
-            p = peer(k)
-            remote(
-                rsend.at[c, p], rrecv.at[c, me], rs_sem.at[c, k], rr_sem.at[c, me], p, s
-            ).start()
+
+        @pl.when(c > 0)
+        def _():
+            give_back(c - 1)
+
         return carry
 
     lax.fori_loop(0, down_steps, down_step, 0)
+    give_back(down_steps - 1)
 
     def sum_step(c, carry):
         for k in range(1, devs):
@@ -559,9 +587,14 @@
 
     lax.fori_loop(0, down_steps, last_step, 0)
     my_rows = pl.ds(pl.multiple_of(me * rows, rows), rows)
-    layer_out[...] = (res32[my_rows, :] + mixture[...]).astype(BF16)
+    residual[...] = res32[my_rows, :]
     for copy in small + att_sends + res_sends + [pair_copy, low_copy]:
         copy.wait_send()
+
+
+def add_kernel(residual, mixture, layer_out, mixture_out):
+    mixture_out[...] = mixture[...]
+    layer_out[...] = (residual[...] + mixture[...]).astype(BF16)
 
 
 def fits(mesh, shapes):
@@ -579,6 +612,7 @@
         and width % units == 0
         and width % (2 * CHUNK) == 0
         and devs % router[1] == 0
+        and devs % NEAR == 0
     )
 
 
@@ -639,6 +673,7 @@
         pltpu.VMEM((all_rows, rank), F32),
         pltpu.VMEM((all_rows, rank), F32),
         pltpu.VMEM((all_rows, units), BF16),
+        pltpu.VMEM((2, all_rows, CHUNK), F32),
         pltpu.VMEM((down_steps, all_rows, CHUNK), BF16),
         pltpu.VMEM((down_steps, all_rows, CHUNK), BF16),
         pltpu.VMEM((down_steps, devs, rows, CHUNK), BF16),
@@ -650,16 +685,16 @@
     scratch += [dma((2,)), dma((2,)), dma((down_steps,)), dma((down_steps,))]
     scratch += [dma((down_steps, devs)), dma((down_steps, devs))]
     scratch += [dma((down_steps,)), dma((down_steps,))]
-    return pl.pallas_call(
+    residual, mixture = pl.pallas_call(
         functools.partial(layer_kernel, devs, subs, slots),
         out_shape=(
-            jax.ShapeDtypeStruct((rows, width), BF16),
+            jax.ShapeDtypeStruct((rows, width), F32),
             jax.ShapeDtypeStruct((rows, width), F32),
         ),
         in_specs=[anywhere] * 4
         + [smem, anywhere, vmem, vmem]
         + [anywhere] * 6
-        + [vmem],
+        + [smem],
         out_specs=(vmem, vmem),
         scratch_shapes=scratch,
         compiler_params=pltpu.CompilerParams(
@@ -680,8 +715,17 @@
         down_w,
         gate_low,
         up_low,
-        experts,
-    )
+        experts.T,
+    )
+    return pl.pallas_call(
+        add_kernel,
+        out_shape=(
+            jax.ShapeDtypeStruct((rows, width), BF16),
+            jax.ShapeDtypeStruct((rows, width), F32),
+        ),
+        in_specs=[vmem, vmem],
+        out_specs=(vmem, vmem),
+    )(residual, mixture)
 
 
 def solution(mesh):

time: 77.3 us -> 63.7 us (0.82)
  Pallas kernels: 72 us -> 62.9 us
  local copies, waits for them, and re-layouts: 4.5 us -> 0 us
    pallas_call x1, Pallas kernels: 72 us -> 61.2 us  [body(): pl.pallas_call(functools.partial(layer_kernel, devs, subs, slots), out_sh...]
    unnamed x3 -> x0, local copies, waits for them, and re-layouts: 4.5 us -> none
    pallas_call x0 -> x1, Pallas kernels: none -> 1.74 us  [body(): pl.pallas_call(add_kernel, out_shape=(jax.ShapeDtypeStruct((rows, width),...]
where the time goes in v2:
time: 63.7 us; the launch traced here: 63.6 us
  Pallas kernels  62.9 us (99%)
  between operations  0.64 us (1%)
    pallas_call x1, Pallas kernels, body(): pl.pallas_call(functools.partial(layer_kernel, devs, subs, slots), out_sh...  61.2 us
    pallas_call x1, Pallas kernels, body(): pl.pallas_call(add_kernel, out_shape=(jax.ShapeDtypeStruct((rows, width),...  1.74 us

profile of v2, /device:TPU:0, one launch (start us, length us, event | category | flops | bytes accessed | tf_op | source)
XLA Modules:
  0.0 63.6 jit_solution(2486338047816335894)
XLA Ops:
  0.6 61.2 %shard_map.158 = (f32[8,6144]{1,0:T(8,128)}, f32[8,6144]{1,0:T(8,128)}) custom-call(bf16[8,6144]{1,0:T(8,128)(2,1)} %hidden.1, bf16[8,24,128]{2,1,0:T(8,128)(2,1)} %query.1, bf16[8,4,64,128]{3,2,1,0:T(8,128)(2,1)} %keys.1, bf16[8,4,64,128]{3,2,1,0:T(8,128)(2,1)} %values.1, s32[8]{0:T(128)} %lengths.1, bf16[3072,768]{1,0:T(8,128)(2,1)} %out_proj.1, ...), custom_call_target="tpu_custom_call" | custom-call | tf_op jit(solution)/shard_map/pallas_call | solution.py:688
  61.8 1.7 %shard_map.159 = (bf16[8,6144]{1,0:T(8,128)(2,1)}, f32[8,6144]{1,0:T(8,128)}) custom-call(f32[8,6144]{1,0:T(8,128)} %get-tuple-element.4.residual, f32[8,6144]{1,0:T(8,128)} %get-tuple-element.5.mixture), custom_call_target="tpu_custom_call" | custom-call | tf_op jit(solution)/shard_map/pallas_call | solution.py:720
